TPU v7x, 32 devices: a whole 2x2x4 slice. The times are simulated.
32 devices in a mesh: groups: 2 (over y), expert: 8 (over z, core), section: 2 (over x), tensor: 1.
Axes of the slice: x: 2, y: 2, z: 4, core: 2. Of those that a mesh axis runs over, the one named last changes fastest.
Arguments:
- opening_residual: bfloat16 [2, 2048, 2048], P('section', ('groups', 'expert'), 'tensor'), parts along dimension 1, may hold values from -12 to 12
- incoming_residual: bfloat16 [1, 2048, 2048], P(None, ('groups', 'expert'), 'tensor'), parts along dimension 1, may hold values from -12 to 12
- stored_summaries: bfloat16 [2, 2, 16, 768, 512], P(None, 'section', ('groups', 'expert')), parts along dimension 2, may hold values from -40 to 40
- stored_counts: int32 [3, 16], P(None, ('groups', 'expert')), parts along dimension 1, may hold values from 1 to 768, as said below
- picked_specialists: int32 [2, 2, 2048, 6], P(None, 'section', ('groups', 'expert')), parts along dimension 2, may hold values from 0 to 15, all different within a row; in each aligned block of 128 rows (0 to 127, 128 to 255, ..., all dimensions but the last counted through in order) at most 64 rows name the same one
- chooser_mixing_share: float32 [2, 2, 2048, 6], P(None, 'section', ('groups', 'expert')), parts along dimension 2, may hold values from 0.05 to 0.4
- mixing_scale_factor: float32 [2, 2048], P('section'), may hold values from 0.25 to 1.75
- asking_projection: bfloat16 [2, 2048, 1024], P('section', None, 'tensor'), may hold values from -0.125 to 0.125
- summary_lookup_factor: bfloat16 [2, 8, 128, 512], P('section', 'tensor'), may hold values from -0.5 to 0.5
- summary_content_factor: bfloat16 [2, 8, 512, 128], P('section', 'tensor'), may hold values from -0.25 to 0.25
- merging_projection: bfloat16 [2, 1024, 2048], P('section', 'tensor'), may hold values from -0.1875 to 0.1875
- compress_projection: bfloat16 [2, 2048, 512], P('section', None, 'tensor'), may hold values from -0.125 to 0.125
- summary_scale_factor: float32 [2, 512], P('section'), may hold values from 0.25 to 1.75
- specialist_scale_factor: float32 [2, 2048], P('section', 'tensor'), may hold values from 0.25 to 1.75
- specialist_switch_factor: bfloat16 [2, 16, 2048, 704], P('section', 'expert', None, 'tensor'), may hold values from -0.125 to 0.125
- specialist_widen_factor: bfloat16 [2, 16, 2048, 704], P('section', 'expert', None, 'tensor'), may hold values from -0.125 to 0.125
- specialist_contract_factor: bfloat16 [2, 16, 704, 2048], P('section', 'expert', 'tensor'), may hold values from -0.21875 to 0.21875
Outputs:
- results: bfloat16 [2, 2, 2048, 2048], P(None, 'section', ('groups', 'expert'), 'tensor'), parts along dimension 2
There are 2 independent parts, one for each index of `groups`. A program takes and returns all parts, laid end to end along the dimension named above; an argument that names none is the same for every part. Nothing has to cross between parts.
Inputs may be any that keep to these rules, and one draw needn't show every extreme that they name: `picked_specialists`: in each aligned block of 128 rows (one sequence) no expert is chosen by more than 64 rows, a bound that some block reaches; each row names 6 different experts. `stored_counts`: in every microbatch some sequence has exactly 768 cached tokens.
All inputs are finite; a program needn't handle non-finite values.
Results may differ from a plain program's by a relative error of at most 0.04.
Values may be sent and summed in bfloat16 or wider, within the bound.
A program may use at most 128 MiB of HBM per device.

v0:
```python
import jax
import jax.numpy as jnp
from jax import lax
from jax.sharding import PartitionSpec as P

CAP = 64
RETURN_CHUNKS = 2
epsilon = 1e-06


def shifted(value, axis, steps):
    count = lax.axis_size(axis)
    initial, last = (max(0, -steps), min(count, count - steps))
    return lax.ppermute(value, axis, [(source, source + steps) for source in range(initial, last)])


def row_norm(values, gain_row):
    return (
        values * lax.rsqrt(jnp.mean(values * values, axis=-1, keepdims=True) + epsilon) * gain_row
    )


def attend(q_lat, cache_rows, new_rows, length, score_scale):
    piece_list = q_lat.shape[0]
    context = cache_rows.shape[0]
    key_rows = jnp.concatenate([cache_rows, new_rows], axis=0)
    scores = (
        jnp.einsum("thl,kl->thk", q_lat, key_rows, preferred_element_type=jnp.float32) * score_scale
    )
    position = lax.broadcasted_iota(jnp.int32, (piece_list, context + piece_list), 1)
    query_pos = lax.broadcasted_iota(jnp.int32, (piece_list, context + piece_list), 0)
    visible = jnp.where(position < context, position < length, position - context <= query_pos)
    scores = jnp.where(visible[:, None, :], scores, -jnp.inf)
    row_max = jnp.max(scores, axis=-1, keepdims=True)
    expd = jnp.where(visible[:, None, :], jnp.exp(scores - row_max), 0.0)
    attention = (expd / jnp.sum(expd, axis=-1, keepdims=True)).astype(jnp.bfloat16)
    return jnp.einsum(
        "thk,kl->thl", attention, key_rows, preferred_element_type=jnp.float32
    ).astype(jnp.bfloat16)


def shards(
    opening_residual,
    incoming_residual,
    stored_summaries,
    stored_counts,
    picked_specialists,
    chooser_mixing_share,
    mixing_scale_factor,
    asking_projection,
    summary_lookup_factor,
    summary_content_factor,
    merging_projection,
    compress_projection,
    summary_scale_factor,
    specialist_scale_factor,
    specialist_switch_factor,
    specialist_widen_factor,
    specialist_contract_factor,
):
    segment_ordinal = lax.axis_index("section")
    section_count = lax.axis_size("section")
    sources = lax.axis_size("expert")
    tick_count = stored_summaries.shape[0]
    piece_list = opening_residual.shape[1]
    inner_feature_midcount = opening_residual.shape[2]
    full_width = mixing_scale_factor.shape[1]
    local_heads = summary_lookup_factor.shape[1]
    head_size = summary_lookup_factor.shape[2]
    top_count = picked_specialists.shape[3]
    expert_local = specialist_switch_factor.shape[1]
    score_scale = head_size ** (-0.5)
    expert_ids = lax.broadcasted_iota(jnp.int32, (1, 1, 1, expert_local * sources), 3)
    shares_dense = jnp.sum(
        jnp.where(
            picked_specialists[:, 0][..., None] == expert_ids,
            chooser_mixing_share[:, 0][..., None],
            0.0,
        ),
        axis=2,
    )
    shares_all = lax.all_gather(jnp.swapaxes(shares_dense, 1, 2), "expert", axis=1, tiled=False)
    mine = lax.dynamic_slice_in_dim(
        shares_all, lax.axis_index("expert") * expert_local, expert_local, axis=2
    )
    chosen = mine > 0.0
    earlier_or_same = (
        lax.broadcasted_iota(jnp.int32, (piece_list, piece_list), 0)
        <= lax.broadcasted_iota(jnp.int32, (piece_list, piece_list), 1)
    ).astype(jnp.bfloat16)
    rank = jnp.einsum(
        "tjer,rq->tjeq",
        chosen.astype(jnp.bfloat16),
        earlier_or_same,
        preferred_element_type=jnp.float32,
    ).astype(jnp.int32)
    slots = lax.broadcasted_iota(jnp.int32, (1, 1, 1, CAP, 1), 3) + 1
    at_slot = (rank[..., None, :] == slots) & chosen[..., None, :]
    placed = at_slot.astype(jnp.bfloat16)
    slot_share = jnp.sum(jnp.where(at_slot, mine[..., None, :], 0.0), axis=-1)
    outputs = []
    present_carry = opening_residual[0]
    section_out = present_carry
    for step_index in range(tick_count):
        if step_index > 0:
            handed = shifted(section_out, "section", 1)
            present_carry = jnp.where(
                segment_ordinal == 0, incoming_residual[step_index - 1], handed
            )
        micro_index = step_index - segment_ordinal + section_count - 1
        length = lax.dynamic_index_in_dim(stored_counts[:, 0], micro_index, 0, keepdims=False)
        full_rows = lax.all_gather(present_carry, "tensor", axis=1, tiled=True)
        normed = row_norm(full_rows.astype(jnp.float32), mixing_scale_factor[0]).astype(
            jnp.bfloat16
        )
        queries = jnp.dot(normed, asking_projection[0], preferred_element_type=jnp.float32).astype(
            jnp.bfloat16
        )
        queries = queries.reshape(piece_list, local_heads, head_size)
        q_lat = jnp.einsum(
            "thd,hdl->thl", queries, summary_lookup_factor[0], preferred_element_type=jnp.float32
        ).astype(jnp.bfloat16)
        latent_part = jnp.dot(normed, compress_projection[0], preferred_element_type=jnp.float32)
        latent_raw = lax.all_gather(
            latent_part.astype(jnp.bfloat16), "tensor", axis=1, tiled=True
        ).astype(latent_part.dtype)
        new_latent = row_norm(latent_raw, summary_scale_factor[0]).astype(jnp.bfloat16)
        o_lat = attend(q_lat, stored_summaries[step_index, 0, 0], new_latent, length, score_scale)
        heads_out = jnp.einsum(
            "thl,hld->thd", o_lat, summary_content_factor[0], preferred_element_type=jnp.float32
        ).astype(jnp.bfloat16)
        heads_out = heads_out.reshape(piece_list, local_heads * head_size)
        head_terms = jnp.dot(heads_out, merging_projection[0], preferred_element_type=jnp.float32)
        residual = present_carry.astype(jnp.float32) + lax.psum_scatter(
            head_terms.astype(jnp.bfloat16), "tensor", scatter_dimension=1, tiled=True
        ).astype(jnp.float32)
        squares = lax.psum(jnp.sum(residual * residual, axis=1), "tensor")
        moe_input = (
            residual
            * lax.rsqrt(squares / full_width + epsilon)[:, None]
            * specialist_scale_factor[0]
        ).astype(jnp.bfloat16)
        whole_rows = lax.all_gather(moe_input, "tensor", axis=1, tiled=True)
        place = placed[step_index]
        share = slot_share[step_index]
        all_rows = lax.all_gather(whole_rows, "expert", axis=0, tiled=True)
        all_rows = all_rows.reshape(sources, piece_list, full_width)
        hidden_list = []
        for e in range(expert_local):
            rows_in = jnp.einsum(
                "jsr,jrd->jsd", place[:, e], all_rows, preferred_element_type=jnp.float32
            ).astype(jnp.bfloat16)
            rows_in = rows_in.reshape(sources * CAP, full_width)
            gate_values = jnp.dot(
                rows_in, specialist_switch_factor[0, e], preferred_element_type=jnp.float32
            )
            up_values = jnp.dot(
                rows_in, specialist_widen_factor[0, e], preferred_element_type=jnp.float32
            )
            hidden_list.append(
                (jax.nn.silu(gate_values) * up_values * share[:, e].reshape(-1, 1)).astype(
                    jnp.bfloat16
                )
            )
        chunk = full_width // RETURN_CHUNKS
        routed_list = []
        for c in range(RETURN_CHUNKS):
            total = None
            for e in range(expert_local):
                down = jnp.dot(
                    hidden_list[e],
                    specialist_contract_factor[0, e][:, c * chunk : (c + 1) * chunk],
                    preferred_element_type=jnp.float32,
                ).astype(jnp.bfloat16)
                term = jnp.einsum(
                    "jsr,jsd->jrd",
                    place[:, e],
                    down.reshape(sources, CAP, chunk),
                    preferred_element_type=jnp.float32,
                )
                total = term if total is None else total + term
            total = total.astype(jnp.bfloat16).reshape(sources * piece_list, chunk)
            routed_list.append(lax.psum_scatter(total, "expert", scatter_dimension=0, tiled=True))
        routed = jnp.concatenate(routed_list, axis=1)
        routed = lax.psum_scatter(routed, "tensor", scatter_dimension=1, tiled=True).astype(
            jnp.float32
        )
        section_out = (residual + routed).astype(jnp.bfloat16)
        outputs.append(section_out)
    return jnp.stack(outputs)[:, None]


def solution(mesh):
    in_specs = (
        P("section", ("groups", "expert"), "tensor"),
        P(None, ("groups", "expert"), "tensor"),
        P(None, "section", ("groups", "expert"), None, None),
        P(None, ("groups", "expert")),
        P(None, "section", ("groups", "expert"), None),
        P(None, "section", ("groups", "expert"), None),
        P("section", None),
        P("section", None, "tensor"),
        P("section", "tensor", None, None),
        P("section", "tensor", None, None),
        P("section", "tensor", None),
        P("section", None, "tensor"),
        P("section", None),
        P("section", "tensor"),
        P("section", "expert", None, "tensor"),
        P("section", "expert", None, "tensor"),
        P("section", "expert", "tensor", None),
    )
    out_specs = P(None, "section", ("groups", "expert"), "tensor")
    return jax.shard_map(shards, mesh=mesh, in_specs=in_specs, out_specs=out_specs, check_vma=False)
```

profile of v0, /device:TPU:0, one launch (start us, length us, event | category | flops | bytes accessed | tf_op | source)
XLA Modules:
  0.0 368.0 jit_solution(13593333180121278280)
XLA Ops:
  6.6 0.6 iota_compare_fusion.5
  7.2 1.4 fusion.145
  8.6 2.2 multiply_reduce_fusion.3
  11.4 3.0 fusion.130
  14.4 1.3 slice_bitcast_fusion.2
  15.7 0.6 constant_dynamic-slice_fusion
  16.3 1.2 iota_compare_fusion.3
  17.5 1.0 multiply_convert_fusion.3
  18.5 1.5 fusion.159
  20.1 4.5 %fusion.105 = f32[128,8,896]{2,0,1:T(8,128)} fusion(bf16[1,8,128,512]{3,2,1,0:T(8,128)(2,1)S(1)} %copy-done.7, bf16[128,512]{1,0:T(8,128)(2,1)S(1)} %multiply_convert_fusion.3, bf16[768,512]{1,0:T(8,128)(2,1)} %get-tuple-element.10, bf16[16,8,8,128]{3,2,1,0:T(8,128)(2,1)S(1)} %fusion.130), kind=kOutput, calls=%fused_computation.97 | convolution fusion | flops 1076101120 | bytes 5898240 | tf_op jit(solution)/shard_map/thl,kl->thk/dot_general | solution.py:28
  24.6 6.7 %fusion.191 = (f32[128,8]{0,1:T(8,128)S(1)}, f32[128,8,896]{2,0,1:T(8,128)}) fusion(f32[128,8,896]{2,0,1:T(8,128)} %fusion.105, pred[128,896]{1,0:T(8,128)(4,1)} %get-tuple-element.20), kind=kOutput, calls=%fused_computation.204 | output fusion | flops 6423423 | bytes 7458816 | tf_op jit(solution)/shard_map/sub | solution.py:35
  31.3 3.9 %fusion.126 = bf16[8,128,128]{1,2,0:T(8,128)(2,1)S(1)} fusion(f32[128,8,896]{2,0,1:T(8,128)} %get-tuple-element.26, f32[128,8]{0,1:T(8,128)S(1)} %get-tuple-element.25, bf16[1,8,512,128]{3,2,1,0:T(8,128)(2,1)} %param.26, bf16[128,512]{1,0:T(8,128)(2,1)S(1)} %multiply_convert_fusion.3, bf16[768,512]{1,0:T(8,128)(2,1)S(1)} %copy-done.10), kind=kOutput, calls=%fused_computation.116 | convolution fusion | flops 1078067200 | bytes 5902336 | tf_op jit(solution)/shard_map/thl,hld->thd/dot_general | solution.py:129
  35.3 3.1 multiply_reduce_fusion.1
  38.5 1.0 multiply_convert_fusion.1
  39.6 16.3 %all-gather = f32[2,128,128]{2,1,0:T(8,128)S(1)} all-gather(f32[2,16,128]{2,1,0:T(8,128)S(1)} %bitcast.305), channel_id=2, replica_groups=mesh['groups'=2,'expert'=8,'section'=2,'tensor'=1] {'expert'}, dimensions={1}, use_global_device_ids=true | all-gather | bytes 147456 | tf_op jit(solution)/shard_map/all_gather | solution.py:82
  56.6 0.6 fusion.189
  57.6 6.3 %slice_bitcast_fusion = (bf16[704,2048]{1,0:T(8,128)(2,1)}, bf16[704,2048]{1,0:T(8,128)(2,1)}) fusion(bf16[1,2,704,2048]{3,2,1,0:T(8,128)(2,1)} %param.33), kind=kLoop, calls=%fused_computation.40 | loop fusion | bytes 11534336 | tf_op jit(solution)/shard_map/squeeze | solution.py:172
  64.0 25.8 %all-gather.4.cloned.1.call-done = bf16[1024,2048]{1,0:T(8,128)(2,1)} async-done(((bf16[128,2048]{1,0:T(8,128)(2,1)}), bf16[1024,2048]{1,0:T(8,128)(2,1)}) %all-gather.4.cloned.1.call-update) | async-done | bytes 4194320 | tf_op jit(solution)/shard_map/all_gather | solution.py:146
  89.8 3.0 convolution_convert_fusion.2
  93.2 0.7 convolution_convert_fusion.3
  93.9 3.9 %fusion.16 = f32[512,704]{0,1:T(8,128)S(1)} fusion(bf16[512,2048]{1,0:T(8,128)(2,1)S(1)} %bitcast.286, bf16[1,2,2048,704]{2,3,1,0:T(8,128)(2,1)} %param.31), kind=kOutput, calls=%fused_computation.30 | convolution fusion | flops 1476395008 | bytes 6422528 | tf_op jit(solution)/shard_map/dot_general | solution.py:154
  97.9 1.7 fusion.24
  99.6 1.9 fusion.92
  101.5 1.0 convolution_convert_fusion.12
  102.5 0.8 fusion.174
  103.3 1.9 fusion.98
  105.2 1.0 convolution_convert_fusion.11
  106.2 2.4 add_convert_fusion.3
  108.7 2.7 convolution_convert_fusion.9
  111.4 1.0 convolution_convert_fusion.10
  112.4 0.8 fusion.173
  113.2 2.1 add_convert_fusion.2
  115.4 27.9 %reduce-scatter.5.cloned.1.call-done = bf16[128,1024]{1,0:T(8,128)(2,1)} async-done(((bf16[1024,1024]{1,0:T(8,128)(2,1)}), bf16[128,1024]{1,0:T(8,128)(2,1)}) %reduce-scatter.5.cloned.1.call-update) | async-done | bytes 262160 | tf_op jit(solution)/shard_map/reduce_scatter | solution.py:183
  143.3 36.7 %reduce-scatter.7.cloned.1.call-done = bf16[128,1024]{1,0:T(8,128)(2,1)} async-done(((bf16[1024,1024]{1,0:T(8,128)(2,1)}), bf16[128,1024]{1,0:T(8,128)(2,1)}) %reduce-scatter.7.cloned.1.call-update) | async-done | bytes 262160 | tf_op jit(solution)/shard_map/reduce_scatter | solution.py:183
  180.0 1.9 add_convert_fusion.5
  182.0 3.4 collective-permute-start
  185.4 8.5 %collective-permute-done = bf16[128,2048]{1,0:T(8,128)(2,1)S(1)} collective-permute-done((bf16[128,2048]{1,0:T(8,128)(2,1)}, bf16[128,2048]{1,0:T(8,128)(2,1)S(1)}, u32[]{:S(2)}, u32[]{:S(2)}) %collective-permute-start) | collective-permute-done | bytes 524320 | tf_op jit(solution)/shard_map/ppermute | solution.py:14
  193.9 1.3 fusion.148
  195.3 3.2 fusion.127
  198.4 0.6 multiply_reduce_fusion.2
  199.7 4.5 %fusion.107 = f32[128,8,896]{2,0,1:T(8,128)} fusion(bf16[1,8,128,512]{3,2,1,0:T(8,128)(2,1)S(1)} %copy-done.8, bf16[128,512]{1,0:T(8,128)(2,1)S(1)} %multiply_convert_fusion.2, bf16[768,512]{1,0:T(8,128)(2,1)} %get-tuple-element.9, bf16[16,8,8,128]{3,2,1,0:T(8,128)(2,1)S(1)} %fusion.127), kind=kOutput, calls=%fused_computation.99 | convolution fusion | flops 1076101120 | bytes 5898240 | tf_op jit(solution)/shard_map/thl,kl->thk/dot_general | solution.py:28
  204.2 6.7 %fusion.192 = (f32[128,8]{0,1:T(8,128)S(1)}, f32[128,8,896]{2,0,1:T(8,128)}) fusion(f32[128,8,896]{2,0,1:T(8,128)} %fusion.107, pred[128,896]{1,0:T(8,128)(4,1)S(1)} %copy-done.18), kind=kOutput, calls=%fused_computation.205 | output fusion | flops 6423423 | bytes 7458816 | tf_op jit(solution)/shard_map/sub | solution.py:35
  211.0 3.7 %fusion.125 = bf16[8,128,128]{1,2,0:T(8,128)(2,1)S(1)} fusion(f32[128,8,896]{2,0,1:T(8,128)} %get-tuple-element.32, f32[128,8]{0,1:T(8,128)S(1)} %get-tuple-element.31, bf16[1,8,512,128]{3,2,1,0:T(8,128)(2,1)S(1)} %copy-done.28, bf16[128,512]{1,0:T(8,128)(2,1)S(1)} %multiply_convert_fusion.2, bf16[768,512]{1,0:T(8,128)(2,1)S(1)} %copy-done.9), kind=kOutput, calls=%fused_computation.115 | convolution fusion | flops 1078067200 | bytes 5902336 | tf_op jit(solution)/shard_map/thl,hld->thd/dot_general | solution.py:129
  214.7 3.0 multiply_reduce_fusion
  217.7 1.0 multiply_convert_fusion
  219.1 48.1 %all-gather.6.cloned.1.call-done = bf16[1024,2048]{1,0:T(8,128)(2,1)} async-done(((bf16[128,2048]{1,0:T(8,128)(2,1)}), bf16[1024,2048]{1,0:T(8,128)(2,1)}) %all-gather.6.cloned.1.call-update) | async-done | bytes 4194320 | tf_op jit(solution)/shard_map/all_gather | solution.py:146
  267.2 3.0 convolution_convert_fusion
  270.7 0.7 convolution_convert_fusion.1
  271.4 3.6 fusion.14
  275.1 1.9 fusion.101
  277.0 1.0 convolution_convert_fusion.6
  278.0 1.8 fusion.22
  279.8 1.9 fusion.95
  281.8 1.0 convolution_convert_fusion.7
  282.8 0.8 fusion.176
  283.6 2.2 add_convert_fusion.1
  286.1 2.5 convolution_convert_fusion.4
  288.6 1.0 convolution_convert_fusion.5
  289.7 0.8 fusion.175
  290.4 2.1 add_convert_fusion
  292.6 28.2 %reduce-scatter.9.cloned.1.call-done = bf16[128,1024]{1,0:T(8,128)(2,1)} async-done(((bf16[1024,1024]{1,0:T(8,128)(2,1)}), bf16[128,1024]{1,0:T(8,128)(2,1)}) %reduce-scatter.9.cloned.1.call-update) | async-done | bytes 262160 | tf_op jit(solution)/shard_map/reduce_scatter | solution.py:183
  320.8 36.9 %reduce-scatter.11.cloned.1.call-done = bf16[128,1024]{1,0:T(8,128)(2,1)} async-done(((bf16[1024,1024]{1,0:T(8,128)(2,1)}), bf16[128,1024]{1,0:T(8,128)(2,1)}) %reduce-scatter.11.cloned.1.call-update) | async-done | bytes 262160 | tf_op jit(solution)/shard_map/reduce_scatter | solution.py:183
  357.7 1.1 fusion.157
  358.8 2.1 maximum_bitcast_fusion
  (130 shorter events, 4.2 us)
Async XLA Ops:
  6.5 2.0 copy-start
  6.5 4.8 %copy-start.4 = (bf16[1,128,2048]{2,1,0:T(8,128)(2,1)S(1)}, bf16[1,128,2048]{2,1,0:T(8,128)(2,1)}, u32[]{:S(2)}) copy-start(bf16[1,128,2048]{2,1,0:T(8,128)(2,1)} %param.17) | copy-start | bytes 1572868
  6.5 4.8 %copy-start.19 = (f32[1,2048]{1,0:T(1,128)S(1)}, f32[1,2048]{1,0:T(1,128)}, u32[]{:S(2)}) copy-start(f32[1,2048]{1,0:T(1,128)} %param.23) | copy-start | bytes 24580
  6.5 83.2 %all-gather.4.cloned.1.call-start = ((), (), s32[]{:S(2)}) async-start(), calls=%async_computation.4 | async-start | bytes 4718592 | tf_op jit(solution)/shard_map/all_gather | solution.py:146
  10.8 3.5 copy-start.17
  11.3 4.3 %copy-start.27 = (s32[3,1]{0,1:T(1,128)S(1)}, s32[3,1]{0,1:T(1,128)}, u32[]{:S(2)}) copy-start(s32[3,1]{0,1:T(1,128)} %param.20) | copy-start | bytes 40
  11.3 6.1 %copy-start.23 = (f32[1,512]{1,0:T(1,128)S(1)}, f32[1,512]{1,0:T(1,128)}, u32[]{:S(2)}) copy-start(f32[1,512]{1,0:T(1,128)} %param.29) | copy-start | bytes 6148
  14.3 5.7 %copy-start.7 = (bf16[1,8,128,512]{3,2,1,0:T(8,128)(2,1)S(1)}, bf16[1,8,128,512]{3,2,1,0:T(8,128)(2,1)}, u32[]{:S(2)}) copy-start(bf16[1,8,128,512]{3,2,1,0:T(8,128)(2,1)} %param.25) | copy-start | bytes 3145732
  24.6 6.7 %copy-start.10 = (bf16[768,512]{1,0:T(8,128)(2,1)S(1)}, bf16[768,512]{1,0:T(8,128)(2,1)}, u32[]{:S(2)}) copy-start(bf16[768,512]{1,0:T(8,128)(2,1)} %get-tuple-element.10) | copy-start | bytes 2359300
  35.3 3.2 copy-start.20
  35.3 4.2 %copy-start.25 = (s32[2,1,128,6]{2,1,3,0:T(1,128)S(1)}, s32[2,1,128,6]{2,1,3,0:T(1,128)}, u32[]{:S(2)}) copy-start(s32[2,1,128,6]{2,1,3,0:T(1,128)} %param.21) | copy-start | bytes 18436
  35.3 4.2 %copy-start.26 = (f32[2,1,128,6]{2,1,3,0:T(1,128)S(1)}, f32[2,1,128,6]{2,1,3,0:T(1,128)}, u32[]{:S(2)}) copy-start(f32[2,1,128,6]{2,1,3,0:T(1,128)} %param.22) | copy-start | bytes 18436
  39.5 103.8 %reduce-scatter.5.cloned.1.call-start = ((), (), s32[]{:S(2)}) async-start(), calls=%async_computation.5 | async-start | bytes 2359296 | tf_op jit(solution)/shard_map/reduce_scatter | solution.py:183
  89.8 3.4 copy-start.2
  93.2 4.6 %slice-start = ((s8[5767168]{0:T(1024)(128)(4,1)}), s8[4194304]{0:T(1024)(128)(4,1)S(1)}, s32[]{:S(2)}) async-start(s8[5767168]{0:T(1024)(128)(4,1)} %bitcast.316), calls=%async_computation.10 | async-start | bytes 8388608
  93.9 3.9 %slice-start.1 = ((s8[5767168]{0:T(1024)(128)(4,1)}), s8[1572864]{0:T(1024)(128)(4,1)S(1)}, s32[]{:S(2)}) async-start(s8[5767168]{0:T(1024)(128)(4,1)} %bitcast.316), calls=%async_computation.11 | async-start | bytes 3145728
  93.9 5.6 %slice-start.4 = ((s8[5767168]{0:T(1024)(128)(4,1)}), s8[4194304]{0:T(1024)(128)(4,1)S(1)}, s32[]{:S(2)}) async-start(s8[5767168]{0:T(1024)(128)(4,1)} %bitcast.320), calls=%async_computation.14 | async-start | bytes 8388608
  97.8 1.7 slice-start.5
  99.6 1.9 copy-start.11
  101.5 1.0 copy-start.29
  103.3 1.9 copy-start.15
  105.2 1.0 copy-start.35
  108.6 71.4 %reduce-scatter.7.cloned.1.call-start = ((), (), s32[]{:S(2)}) async-start(), calls=%async_computation.6 | async-start | bytes 2359296 | tf_op jit(solution)/shard_map/reduce_scatter | solution.py:183
  108.6 2.8 copy-start.12
  108.6 2.8 copy-start.30
  115.3 151.9 %all-gather.6.cloned.1.call-start = ((), (), s32[]{:S(2)}) async-start(), calls=%async_computation.7 | async-start | bytes 4718592 | tf_op jit(solution)/shard_map/all_gather | solution.py:146
  182.0 12.0 %collective-permute-start = (bf16[128,2048]{1,0:T(8,128)(2,1)}, bf16[128,2048]{1,0:T(8,128)(2,1)S(1)}, u32[]{:S(2)}, u32[]{:S(2)}) collective-permute-start(bf16[128,2048]{1,0:T(8,128)(2,1)} %add_convert_fusion.5), channel_id=1, source_target_pairs={{0,1},{2,3},{4,5},{6,7},{8,9},{10,11},{12,13},{14,15},{16,17},{18,... | collective-permute-start | bytes 1572872 | tf_op jit(solution)/shard_map/ppermute | solution.py:14
  195.2 3.8 %copy-start.5 = (bf16[128,2048]{1,0:T(8,128)(2,1)}, bf16[128,2048]{1,0:T(8,128)(2,1)S(1)}, u32[]{:S(2)}) copy-start(bf16[128,2048]{1,0:T(8,128)(2,1)S(1)} %get-tuple-element.6) | copy-start | bytes 1572868
  195.3 3.8 %copy-start.24 = (f32[1,512]{1,0:T(1,128)S(1)}, f32[1,512]{1,0:T(1,128)}, u32[]{:S(2)}) copy-start(f32[1,512]{1,0:T(1,128)} %param.29) | copy-start | bytes 6148
  198.4 1.2 copy-start.8
  199.7 4.5 %copy-start.18 = (pred[128,896]{1,0:T(8,128)(4,1)S(1)}, pred[128,896]{1,0:T(8,128)(4,1)}, u32[]{:S(2)}) copy-start(pred[128,896]{1,0:T(8,128)(4,1)} %get-tuple-element.19) | copy-start | bytes 344068
  204.2 6.8 %copy-start.9 = (bf16[768,512]{1,0:T(8,128)(2,1)S(1)}, bf16[768,512]{1,0:T(8,128)(2,1)}, u32[]{:S(2)}) copy-start(bf16[768,512]{1,0:T(8,128)(2,1)} %get-tuple-element.9) | copy-start | bytes 2359300
  204.2 6.8 %copy-start.28 = (bf16[1,8,512,128]{3,2,1,0:T(8,128)(2,1)S(1)}, bf16[1,8,512,128]{3,2,1,0:T(8,128)(2,1)}, u32[]{:S(2)}) copy-start(bf16[1,8,512,128]{3,2,1,0:T(8,128)(2,1)} %param.26) | copy-start | bytes 3145732
  210.9 3.7 %copy-start.6 = (bf16[128,2048]{1,0:T(8,128)(2,1)S(1)}, bf16[128,2048]{1,0:T(8,128)(2,1)}, u32[]{:S(2)}) copy-start(bf16[128,2048]{1,0:T(8,128)(2,1)} %copy-done.5) | copy-start | bytes 1572868
  214.7 4.3 %copy-start.22 = (f32[8,1,64]{2,0,1:T(8,128)S(1)}, f32[8,1,64]{2,0,1:T(8,128)}, u32[]{:S(2)}) copy-start(f32[8,1,64]{2,0,1:T(8,128)} %get-tuple-element.15) | copy-start | bytes 6148
  214.7 4.4 %copy-start.21 = (f32[8,1,64]{2,0,1:T(8,128)S(1)}, f32[8,1,64]{2,0,1:T(8,128)}, u32[]{:S(2)}) copy-start(f32[8,1,64]{2,0,1:T(8,128)} %get-tuple-element.16) | copy-start | bytes 6148
  218.7 102.1 %reduce-scatter.9.cloned.1.call-start = ((), (), s32[]{:S(2)}) async-start(), calls=%async_computation.8 | async-start | bytes 2359296 | tf_op jit(solution)/shard_map/reduce_scatter | solution.py:183
  267.2 3.4 copy-start.3
  267.2 7.8 %slice-start.6 = ((s8[5767168]{0:T(1024)(128)(4,1)}), s8[4194304]{0:T(1024)(128)(4,1)S(1)}, s32[]{:S(2)}) async-start(s8[5767168]{0:T(1024)(128)(4,1)} %bitcast.322), calls=%async_computation.16 | async-start | bytes 8388608
  270.7 4.4 %slice-start.7 = ((s8[5767168]{0:T(1024)(128)(4,1)}), s8[1572864]{0:T(1024)(128)(4,1)S(1)}, s32[]{:S(2)}) async-start(s8[5767168]{0:T(1024)(128)(4,1)} %bitcast.322), calls=%async_computation.17 | async-start | bytes 3145728
  271.4 6.6 %slice-start.2 = ((s8[5767168]{0:T(1024)(128)(4,1)}), s8[4194304]{0:T(1024)(128)(4,1)S(1)}, s32[]{:S(2)}) async-start(s8[5767168]{0:T(1024)(128)(4,1)} %bitcast.318), calls=%async_computation.12 | async-start | bytes 8388608
  275.1 1.9 copy-start.16
  275.1 2.9 slice-start.3
  277.0 1.0 copy-start.31
  279.8 2.0 copy-start.13
  281.8 1.0 copy-start.33
  283.6 2.5 copy-start.32
  285.8 71.9 %reduce-scatter.11.cloned.1.call-start = ((), (), s32[]{:S(2)}) async-start(), calls=%async_computation.9 | async-start | bytes 2359296 | tf_op jit(solution)/shard_map/reduce_scatter | solution.py:183
  286.1 2.5 copy-start.14
  286.1 2.5 copy-start.34
  292.5 68.4 %copy-start.1 = (bf16[1,2048,512]{2,1,0:T(8,128)(2,1)S(1)}, bf16[1,2048,512]{2,1,0:T(8,128)(2,1)}, u32[]{:S(2)}) copy-start(bf16[1,2048,512]{2,1,0:T(8,128)(2,1)} %param.28) | copy-start | bytes 6291460
Sparse Core Ops, SparseCore 0:
  39.6 50.1 all-gather.3
  108.7 34.5 reduce-scatter.4
  145.6 34.3 reduce-scatter.6
  218.8 48.3 all-gather.5
  285.9 34.8 reduce-scatter.8
  323.0 34.6 reduce-scatter.10
where the time goes:
time: 374 us; the launch traced here: 368 us
  waiting for transfers between devices  212 us (57%)
  matrix products  81 us (22%)
  other arithmetic  29.1 us (8%)
  blocking collectives  16.3 us (4%)
  between operations  14.6 us (4%)
  local copies, waits for them, and re-layouts  10.7 us (3%)
  starting transfers between devices  4.1 us (1%)
    reduce_scatter x4, waiting for transfers between devices, shards(): lax.psum_scatter(total, 'expert', scatter_dimension=0, tiled=True)  130 us
    all_gather x2, waiting for transfers between devices, shards(): all_rows = lax.all_gather(whole_rows, 'expert', axis=0, tiled=True)  73.9 us
    all_gather x1, blocking collectives, shards(): lax.all_gather(jnp.swapaxes(shares_dense, 1, 2), 'expert', axis=1, tiled=...  16.3 us
    sub x2, other arithmetic, attend(): expd = jnp.where(visible[:, None, :], jnp.exp(scores - row_max), 0.0)  13.5 us
    dot_general x8, matrix products, shards(): jnp.einsum('jsr,jsd->jrd', place[:, e], down.reshape(sources, CAP, chunk)...  11.8 us
    dot_general x8, matrix products, shards(): jnp.dot(hidden_list[e], specialist_contract_factor[0, e][:, c * chunk:(c...  11.2 us
    dot_general x4, matrix products, shards(): jnp.dot(rows_in, specialist_switch_factor[0, e], preferred_element_type=j...  10.9 us
    dot_general x2, matrix products, attend(): jnp.einsum('thl,kl->thk', q_lat, key_rows, preferred_element_type=jnp.flo...  9.03 us
  transfers between devices with their start and end apart: 7, of which 7 were waited for; matrix products, arithmetic and copies ran while one was open for 6% of the time, Pallas kernels for 0%

commit v1 on v0

--- a/solution.py
+++ b/solution.py
@@ -143,7 +143,16 @@
         whole_rows = lax.all_gather(moe_input, "tensor", axis=1, tiled=True)
         place = placed[step_index]
         share = slot_share[step_index]
-        all_rows = lax.all_gather(whole_rows, "expert", axis=0, tiled=True)
+        ring = [whole_rows]
+        for hop in range(7):
+            ring.append(
+                lax.ppermute(ring[-1], "expert", [(dev, (dev + 1) % 8) for dev in range(8)])
+            )
+        all_rows = jnp.roll(
+            jnp.concatenate(ring[::-1], axis=0),
+            (lax.axis_index("expert") + 1) * ring[0].shape[0],
+            axis=0,
+        )
         all_rows = all_rows.reshape(sources, piece_list, full_width)
         hidden_list = []
         for e in range(expert_local):

time: 374 us -> 449 us (1.20)
  waiting for transfers between devices: 212 us -> 270 us
  starting transfers between devices: 4.1 us -> 14.6 us
  matrix products: 81 us -> 71.2 us
  other arithmetic: 29.1 us -> 36.9 us
  local copies, waits for them, and re-layouts: 10.7 us -> 17.3 us
    ppermute x0 -> x14, waiting for transfers between devices: none -> 131 us  [shards(): lax.ppermute(ring[-1], 'expert', [(dev, (dev + 1) % 8) for dev in range(8)])]
    all_gather x2 -> x0, waiting for transfers between devices: 73.9 us -> none  [shards(): all_rows = lax.all_gather(whole_rows, 'expert', axis=0, tiled=True)]
    ppermute x0 -> x14, starting transfers between devices: none -> 10.4 us  [shards(): lax.ppermute(ring[-1], 'expert', [(dev, (dev + 1) % 8) for dev in range(8)])]
    concatenate x0 -> x4, other arithmetic: none -> 9.33 us  [the longest x2 9.02 us: shards(): jnp.roll(jnp.concatenate(ring[::-1], axis=0), (lax.axis_index('expert') +...]
    unnamed x91 -> x111, local copies, waits for them, and re-layouts: 1.52 us -> 10.8 us
    dot_general x4, matrix products: 7.47 us -> 2.82 us  [shards(): jnp.einsum('jsr,jrd->jsd', place[:, e], all_rows, preferred_element_type=...]
  transfers between devices with their start and end apart: 7 -> 19, of which waited for: 7 -> 18; matrix products, arithmetic and copies ran while one was open for 6% -> 4% of each run, Pallas kernels for 0% -> 0%
where the time goes in v1:
time: 449 us; the launch traced here: 442 us
  waiting for transfers between devices  270 us (60%)
  matrix products  71.2 us (16%)
  other arithmetic  36.9 us (8%)
  local copies, waits for them, and re-layouts  17.3 us (4%)
  blocking collectives  17.1 us (4%)
  starting transfers between devices  14.6 us (3%)
  between operations  14.4 us (3%)
    ppermute x14, waiting for transfers between devices, shards(): lax.ppermute(ring[-1], 'expert', [(dev, (dev + 1) % 8) for dev in range(8)])  131 us
    reduce_scatter x4, waiting for transfers between devices, shards(): lax.psum_scatter(total, 'expert', scatter_dimension=0, tiled=True)  130 us
    all_gather x1, blocking collectives, shards(): lax.all_gather(jnp.swapaxes(shares_dense, 1, 2), 'expert', axis=1, tiled=...  17.1 us
    sub x2, other arithmetic, attend(): expd = jnp.where(visible[:, None, :], jnp.exp(scores - row_max), 0.0)  13.5 us
    dot_general x8, matrix products, shards(): jnp.einsum('jsr,jsd->jrd', place[:, e], down.reshape(sources, CAP, chunk)...  11.5 us
    dot_general x8, matrix products, shards(): jnp.dot(hidden_list[e], specialist_contract_factor[0, e][:, c * chunk:(c...  11.3 us
    unnamed x111, local copies, waits for them, and re-layouts  10.8 us
    ppermute x14, starting transfers between devices, shards(): lax.ppermute(ring[-1], 'expert', [(dev, (dev + 1) % 8) for dev in range(8)])  10.4 us
  transfers between devices with their start and end apart: 19, of which 18 were waited for; matrix products, arithmetic and copies ran while one was open for 4% of the time, Pallas kernels for 0%

profile of v1, /device:TPU:0, one launch (start us, length us, event | category | flops | bytes accessed | tf_op | source)
XLA Modules:
  0.0 441.5 jit_solution(5746782567546266638)
XLA Ops:
  7.1 1.4 fusion.147
  8.6 3.2 fusion.132
  11.9 1.2 multiply_reduce_fusion.3
  13.6 1.3 slice_bitcast_fusion.2
  15.5 1.3 iota_compare_fusion.3
  17.9 1.5 fusion.161
  19.4 4.5 %fusion.107 = f32[128,8,896]{2,0,1:T(8,128)} fusion(bf16[1,8,128,512]{3,2,1,0:T(8,128)(2,1)S(1)} %copy-done.5, bf16[128,512]{1,0:T(8,128)(2,1)S(1)} %multiply_convert_fusion.3, bf16[768,512]{1,0:T(8,128)(2,1)} %get-tuple-element.11, bf16[16,8,8,128]{3,2,1,0:T(8,128)(2,1)S(1)} %fusion.132), kind=kOutput, calls=%fused_computation.103 | convolution fusion | flops 1076101120 | bytes 5898240 | tf_op jit(solution)/shard_map/thl,kl->thk/dot_general | solution.py:28
  23.9 6.8 %fusion.193 = (f32[128,8]{0,1:T(8,128)S(1)}, f32[128,8,896]{2,0,1:T(8,128)}) fusion(f32[128,8,896]{2,0,1:T(8,128)} %fusion.107, pred[128,896]{1,0:T(8,128)(4,1)} %get-tuple-element.21), kind=kOutput, calls=%fused_computation.226 | output fusion | flops 6423423 | bytes 7458816 | tf_op jit(solution)/shard_map/sub | solution.py:35
  30.6 3.9 fusion.128
  34.6 3.1 multiply_reduce_fusion.1
  38.5 10.9 %collective-permute-done = bf16[128,2048]{1,0:T(8,128)(2,1)S(1)} collective-permute-done((bf16[128,2048]{1,0:T(8,128)(2,1)S(1)}, bf16[128,2048]{1,0:T(8,128)(2,1)S(1)}, u32[]{:S(2)}, u32[]{:S(2)}) %collective-permute-start) | collective-permute-done | bytes 524320 | tf_op jit(solution)/shard_map/ppermute | solution.py:149
  50.2 10.4 %collective-permute-done.1 = bf16[128,2048]{1,0:T(8,128)(2,1)S(1)} collective-permute-done((bf16[128,2048]{1,0:T(8,128)(2,1)S(1)}, bf16[128,2048]{1,0:T(8,128)(2,1)S(1)}, u32[]{:S(2)}, u32[]{:S(2)}) %collective-permute-start.1) | collective-permute-done | bytes 524320 | tf_op jit(solution)/shard_map/ppermute | solution.py:149
  61.4 10.5 %collective-permute-done.2 = bf16[128,2048]{1,0:T(8,128)(2,1)} collective-permute-done((bf16[128,2048]{1,0:T(8,128)(2,1)S(1)}, bf16[128,2048]{1,0:T(8,128)(2,1)}, u32[]{:S(2)}, u32[]{:S(2)}) %collective-permute-start.2) | collective-permute-done | bytes 524320 | tf_op jit(solution)/shard_map/ppermute | solution.py:149
  72.0 17.1 %all-gather = f32[2,128,128]{2,1,0:T(8,128)S(1)} all-gather(f32[2,16,128]{2,1,0:T(8,128)S(1)} %bitcast.309), channel_id=2, replica_groups=mesh['groups'=2,'expert'=8,'section'=2,'tensor'=1] {'expert'}, dimensions={1}, use_global_device_ids=true | all-gather | bytes 147456 | tf_op jit(solution)/shard_map/all_gather | solution.py:82
  90.0 9.9 %collective-permute-done.4 = bf16[128,2048]{1,0:T(8,128)(2,1)} collective-permute-done((bf16[128,2048]{1,0:T(8,128)(2,1)}, bf16[128,2048]{1,0:T(8,128)(2,1)}, u32[]{:S(2)}, u32[]{:S(2)}) %collective-permute-start.4) | collective-permute-done | bytes 524320 | tf_op jit(solution)/shard_map/ppermute | solution.py:149
  101.0 9.7 %collective-permute-done.5 = bf16[128,2048]{1,0:T(8,128)(2,1)} collective-permute-done((bf16[128,2048]{1,0:T(8,128)(2,1)}, bf16[128,2048]{1,0:T(8,128)(2,1)}, u32[]{:S(2)}, u32[]{:S(2)}) %collective-permute-start.5) | collective-permute-done | bytes 524320 | tf_op jit(solution)/shard_map/ppermute | solution.py:149
  110.7 9.6 %collective-permute-start.6 = (bf16[128,2048]{1,0:T(8,128)(2,1)}, bf16[128,2048]{1,0:T(8,128)(2,1)S(1)}, u32[]{:S(2)}, u32[]{:S(2)}) collective-permute-start(bf16[128,2048]{1,0:T(8,128)(2,1)} %collective-permute-done.5), channel_id=1, source_target_pairs={{0,2},{2,4},{4,6},{6,8},{8,10},{10,12},{12,14},{14,0},{1,3},{3,5},... | collective-permute-start | bytes 1572872 | tf_op jit(solution)/shard_map/ppermute | solution.py:149
  120.3 3.7 slice_bitcast_fusion
  124.0 6.9 %collective-permute-done.6 = bf16[128,2048]{1,0:T(8,128)(2,1)S(1)} collective-permute-done((bf16[128,2048]{1,0:T(8,128)(2,1)}, bf16[128,2048]{1,0:T(8,128)(2,1)S(1)}, u32[]{:S(2)}, u32[]{:S(2)}) %collective-permute-start.6) | collective-permute-done | bytes 524320 | tf_op jit(solution)/shard_map/ppermute | solution.py:149
  130.9 1.1 constant_dynamic-update-slice_fusion.6
  132.0 1.1 constant_dynamic-update-slice_fusion.5
  133.1 1.1 constant_dynamic-update-slice_fusion.4
  134.1 1.1 constant_dynamic-update-slice_fusion.3
  135.5 4.4 %fusion.3 = bf16[1024,2048]{1,0:T(8,128)(2,1)S(1)} fusion(s32[]{:T(128)S(6)} %select_n.80, bf16[1024,2048]{1,0:T(8,128)(2,1)S(1)} %constant_dynamic-update-slice_fusion), kind=kLoop, calls=%fused_computation.7 | loop fusion | flops 8388608 | bytes 8388612 | tf_op jit(solution)/shard_map/jit(_roll_dynamic)/concatenate | solution.py:151
  141.4 1.7 fusion.18
  143.1 1.7 fusion.26
  144.9 1.9 fusion.94
  148.6 1.9 fusion.100
  151.6 2.1 add_convert_fusion.3
  154.2 2.7 convolution_convert_fusion.9
  158.8 2.1 add_convert_fusion.2
  161.0 27.7 %reduce-scatter.5.cloned.1.call-done = bf16[128,1024]{1,0:T(8,128)(2,1)} async-done(((bf16[1024,1024]{1,0:T(8,128)(2,1)}), bf16[128,1024]{1,0:T(8,128)(2,1)}) %reduce-scatter.5.cloned.1.call-update) | async-done | bytes 262160 | tf_op jit(solution)/shard_map/reduce_scatter | solution.py:192
  188.6 37.0 %reduce-scatter.7.cloned.1.call-done = bf16[128,1024]{1,0:T(8,128)(2,1)} async-done(((bf16[1024,1024]{1,0:T(8,128)(2,1)}), bf16[128,1024]{1,0:T(8,128)(2,1)}) %reduce-scatter.7.cloned.1.call-update) | async-done | bytes 262160 | tf_op jit(solution)/shard_map/reduce_scatter | solution.py:192
  225.6 2.0 add_convert_fusion.5
  227.6 3.4 collective-permute-start.7
  231.1 8.7 %collective-permute-done.7 = bf16[128,2048]{1,0:T(8,128)(2,1)S(1)} collective-permute-done((bf16[128,2048]{1,0:T(8,128)(2,1)}, bf16[128,2048]{1,0:T(8,128)(2,1)S(1)}, u32[]{:S(2)}, u32[]{:S(2)}) %collective-permute-start.7) | collective-permute-done | bytes 524320 | tf_op jit(solution)/shard_map/ppermute | solution.py:14
  239.7 1.3 fusion.150
  241.1 3.2 fusion.129
  245.0 4.5 %fusion.109 = f32[128,8,896]{2,0,1:T(8,128)} fusion(bf16[1,8,128,512]{3,2,1,0:T(8,128)(2,1)S(1)} %copy-done.6, bf16[128,512]{1,0:T(8,128)(2,1)S(1)} %multiply_convert_fusion.2, bf16[768,512]{1,0:T(8,128)(2,1)} %get-tuple-element.10, bf16[16,8,8,128]{3,2,1,0:T(8,128)(2,1)S(1)} %fusion.129), kind=kOutput, calls=%fused_computation.105 | convolution fusion | flops 1076101120 | bytes 5898240 | tf_op jit(solution)/shard_map/thl,kl->thk/dot_general | solution.py:28
  249.5 6.7 %fusion.194 = (f32[128,8]{0,1:T(8,128)S(1)}, f32[128,8,896]{2,0,1:T(8,128)}) fusion(f32[128,8,896]{2,0,1:T(8,128)} %fusion.109, pred[128,896]{1,0:T(8,128)(4,1)S(1)} %copy-done.22), kind=kOutput, calls=%fused_computation.227 | output fusion | flops 6423423 | bytes 7458816 | tf_op jit(solution)/shard_map/sub | solution.py:35
  256.2 3.7 fusion.127
  260.0 3.0 multiply_reduce_fusion
  263.3 10.4 %collective-permute-done.8 = bf16[128,2048]{1,0:T(8,128)(2,1)S(1)} collective-permute-done((bf16[128,2048]{1,0:T(8,128)(2,1)S(1)}, bf16[128,2048]{1,0:T(8,128)(2,1)S(1)}, u32[]{:S(2)}, u32[]{:S(2)}) %collective-permute-start.8) | collective-permute-done | bytes 524320 | tf_op jit(solution)/shard_map/ppermute | solution.py:149
  273.6 10.4 %collective-permute-done.9 = bf16[128,2048]{1,0:T(8,128)(2,1)S(1)} collective-permute-done((bf16[128,2048]{1,0:T(8,128)(2,1)S(1)}, bf16[128,2048]{1,0:T(8,128)(2,1)S(1)}, u32[]{:S(2)}, u32[]{:S(2)}) %collective-permute-start.9) | collective-permute-done | bytes 524320 | tf_op jit(solution)/shard_map/ppermute | solution.py:149
  284.1 10.4 %collective-permute-done.10 = bf16[128,2048]{1,0:T(8,128)(2,1)S(1)} collective-permute-done((bf16[128,2048]{1,0:T(8,128)(2,1)S(1)}, bf16[128,2048]{1,0:T(8,128)(2,1)S(1)}, u32[]{:S(2)}, u32[]{:S(2)}) %collective-permute-start.10) | collective-permute-done | bytes 524320 | tf_op jit(solution)/shard_map/ppermute | solution.py:149
  294.5 10.4 %collective-permute-done.11 = bf16[128,2048]{1,0:T(8,128)(2,1)S(1)} collective-permute-done((bf16[128,2048]{1,0:T(8,128)(2,1)S(1)}, bf16[128,2048]{1,0:T(8,128)(2,1)S(1)}, u32[]{:S(2)}, u32[]{:S(2)}) %collective-permute-start.11) | collective-permute-done | bytes 524320 | tf_op jit(solution)/shard_map/ppermute | solution.py:149
  304.9 10.4 %collective-permute-done.12 = bf16[128,2048]{1,0:T(8,128)(2,1)S(1)} collective-permute-done((bf16[128,2048]{1,0:T(8,128)(2,1)S(1)}, bf16[128,2048]{1,0:T(8,128)(2,1)S(1)}, u32[]{:S(2)}, u32[]{:S(2)}) %collective-permute-start.12) | collective-permute-done | bytes 524320 | tf_op jit(solution)/shard_map/ppermute | solution.py:149
  316.1 10.5 %collective-permute-done.13 = bf16[128,2048]{1,0:T(8,128)(2,1)} collective-permute-done((bf16[128,2048]{1,0:T(8,128)(2,1)S(1)}, bf16[128,2048]{1,0:T(8,128)(2,1)}, u32[]{:S(2)}, u32[]{:S(2)}) %collective-permute-start.13) | collective-permute-done | bytes 524320 | tf_op jit(solution)/shard_map/ppermute | solution.py:149
  326.7 10.6 %collective-permute-done.14 = bf16[128,2048]{1,0:T(8,128)(2,1)} collective-permute-done((bf16[128,2048]{1,0:T(8,128)(2,1)}, bf16[128,2048]{1,0:T(8,128)(2,1)}, u32[]{:S(2)}, u32[]{:S(2)}) %collective-permute-start.14) | collective-permute-done | bytes 524320 | tf_op jit(solution)/shard_map/ppermute | solution.py:149
  337.3 1.1 constant_dynamic-update-slice_fusion.15
  338.4 1.1 constant_dynamic-update-slice_fusion.14
  339.4 1.1 constant_dynamic-update-slice_fusion.13
  340.9 4.6 %fusion.2 = bf16[1024,2048]{1,0:T(8,128)(2,1)S(1)} fusion(s32[]{:T(128)S(6)} %select_n.80, bf16[1024,2048]{1,0:T(8,128)(2,1)S(1)} %constant_dynamic-update-slice_fusion.8), kind=kLoop, calls=%fused_computation.6 | loop fusion | flops 8388608 | bytes 8388612 | tf_op jit(solution)/shard_map/jit(_roll_dynamic)/concatenate | solution.py:151
  347.0 1.7 fusion.16
  349.0 1.9 fusion.103
  351.9 1.7 fusion.24
  353.6 1.9 fusion.97
  357.3 2.1 add_convert_fusion
  359.8 2.5 convolution_convert_fusion.6
  364.1 2.1 add_convert_fusion.1
  366.3 28.4 %reduce-scatter.11.cloned.1.call-done = bf16[128,1024]{1,0:T(8,128)(2,1)} async-done(((bf16[1024,1024]{1,0:T(8,128)(2,1)}), bf16[128,1024]{1,0:T(8,128)(2,1)}) %reduce-scatter.11.cloned.1.call-update) | async-done | bytes 262160 | tf_op jit(solution)/shard_map/reduce_scatter | solution.py:192
  394.6 36.9 %reduce-scatter.9.cloned.1.call-done = bf16[128,1024]{1,0:T(8,128)(2,1)} async-done(((bf16[1024,1024]{1,0:T(8,128)(2,1)}), bf16[128,1024]{1,0:T(8,128)(2,1)}) %reduce-scatter.9.cloned.1.call-update) | async-done | bytes 262160 | tf_op jit(solution)/shard_map/reduce_scatter | solution.py:192
  431.5 1.1 fusion.159
  432.7 2.1 maximum_bitcast_fusion
  (176 shorter events, 22.8 us)
Async XLA Ops:
  6.5 5.3 %copy-start = (bf16[1,2048,512]{2,1,0:T(8,128)(2,1)S(1)}, bf16[1,2048,512]{2,1,0:T(8,128)(2,1)}, u32[]{:S(2)}) copy-start(bf16[1,2048,512]{2,1,0:T(8,128)(2,1)} %param.30) | copy-start | bytes 6291460
  6.5 5.3 %copy-start.2 = (bf16[1,128,2048]{2,1,0:T(8,128)(2,1)S(1)}, bf16[1,128,2048]{2,1,0:T(8,128)(2,1)}, u32[]{:S(2)}) copy-start(bf16[1,128,2048]{2,1,0:T(8,128)(2,1)} %param.19) | copy-start | bytes 1572868
  6.5 5.3 %copy-start.23 = (f32[1,2048]{1,0:T(1,128)S(1)}, f32[1,2048]{1,0:T(1,128)}, u32[]{:S(2)}) copy-start(f32[1,2048]{1,0:T(1,128)} %param.25) | copy-start | bytes 24580
  6.5 182.1 %reduce-scatter.5.cloned.1.call-start = ((), (), s32[]{:S(2)}) async-start(), calls=%async_computation.4 | async-start | bytes 2359296 | tf_op jit(solution)/shard_map/reduce_scatter | solution.py:192
  8.6 5.0 %copy-start.15 = (bf16[2,1,1,768,512]{4,3,2,1,0:T(8,128)(2,1)S(1)}, bf16[2,1,1,768,512]{4,3,2,1,0:T(8,128)(2,1)}, u32[]{:S(2)}) copy-start(bf16[2,1,1,768,512]{4,3,2,1,0:T(8,128)(2,1)} %param.21) | copy-start | bytes 4718596
  11.9 3.1 copy-start.30
  11.9 4.9 %copy-start.26 = (f32[1,512]{1,0:T(1,128)S(1)}, f32[1,512]{1,0:T(1,128)}, u32[]{:S(2)}) copy-start(f32[1,512]{1,0:T(1,128)} %param.31) | copy-start | bytes 6148
  13.1 6.3 %copy-start.5 = (bf16[1,8,128,512]{3,2,1,0:T(8,128)(2,1)S(1)}, bf16[1,8,128,512]{3,2,1,0:T(8,128)(2,1)}, u32[]{:S(2)}) copy-start(bf16[1,8,128,512]{3,2,1,0:T(8,128)(2,1)} %param.27) | copy-start | bytes 3145732
  23.9 6.8 %copy-start.8 = (bf16[768,512]{1,0:T(8,128)(2,1)S(1)}, bf16[768,512]{1,0:T(8,128)(2,1)}, u32[]{:S(2)}) copy-start(bf16[768,512]{1,0:T(8,128)(2,1)} %get-tuple-element.11) | copy-start | bytes 2359300
  34.6 3.2 copy-start.21
  34.6 37.3 %copy-start.28 = (s32[2,1,128,6]{2,1,3,0:T(1,128)S(1)}, s32[2,1,128,6]{2,1,3,0:T(1,128)}, u32[]{:S(2)}) copy-start(s32[2,1,128,6]{2,1,3,0:T(1,128)} %param.23) | copy-start | bytes 18436
  34.6 37.3 %copy-start.29 = (f32[2,1,128,6]{2,1,3,0:T(1,128)S(1)}, f32[2,1,128,6]{2,1,3,0:T(1,128)}, u32[]{:S(2)}) copy-start(f32[2,1,128,6]{2,1,3,0:T(1,128)} %param.24) | copy-start | bytes 18436
  37.9 11.4 %collective-permute-start = (bf16[128,2048]{1,0:T(8,128)(2,1)S(1)}, bf16[128,2048]{1,0:T(8,128)(2,1)S(1)}, u32[]{:S(2)}, u32[]{:S(2)}) collective-permute-start(bf16[128,2048]{1,0:T(8,128)(2,1)S(1)} %multiply_convert_fusion.1), channel_id=1, source_target_pairs={{0,2},{2,4},{4,6},{6,8},{8,10},{10,12},{12,14},{14,0},{1,3},{3,5},... | collective-permute-start | bytes 1572872 | tf_op jit(solution)/shard_map/ppermute | solution.py:149
  50.2 10.4 %collective-permute-start.1 = (bf16[128,2048]{1,0:T(8,128)(2,1)S(1)}, bf16[128,2048]{1,0:T(8,128)(2,1)S(1)}, u32[]{:S(2)}, u32[]{:S(2)}) collective-permute-start(bf16[128,2048]{1,0:T(8,128)(2,1)S(1)} %collective-permute-done), channel_id=1, source_target_pairs={{0,2},{2,4},{4,6},{6,8},{8,10},{10,12},{12,14},{14,0},{1,3},{3,5},... | collective-permute-start | bytes 1572872 | tf_op jit(solution)/shard_map/ppermute | solution.py:149
  60.6 0.8 copy-start.18
  61.4 10.5 %collective-permute-start.2 = (bf16[128,2048]{1,0:T(8,128)(2,1)S(1)}, bf16[128,2048]{1,0:T(8,128)(2,1)}, u32[]{:S(2)}, u32[]{:S(2)}) collective-permute-start(bf16[128,2048]{1,0:T(8,128)(2,1)S(1)} %collective-permute-done.1), channel_id=1, source_target_pairs={{0,2},{2,4},{4,6},{6,8},{8,10},{10,12},{12,14},{14,0},{1,3},{3,5},... | collective-permute-start | bytes 1572872 | tf_op jit(solution)/shard_map/ppermute | solution.py:149
  71.9 17.2 %collective-permute-start.3 = (bf16[128,2048]{1,0:T(8,128)(2,1)}, bf16[128,2048]{1,0:T(8,128)(2,1)}, u32[]{:S(2)}, u32[]{:S(2)}) collective-permute-start(bf16[128,2048]{1,0:T(8,128)(2,1)} %collective-permute-done.2), channel_id=1, source_target_pairs={{0,2},{2,4},{4,6},{6,8},{8,10},{10,12},{12,14},{14,0},{1,3},{3,5},... | collective-permute-start | bytes 1572872 | tf_op jit(solution)/shard_map/ppermute | solution.py:149
  89.2 10.8 %collective-permute-start.4 = (bf16[128,2048]{1,0:T(8,128)(2,1)}, bf16[128,2048]{1,0:T(8,128)(2,1)}, u32[]{:S(2)}, u32[]{:S(2)}) collective-permute-start(bf16[128,2048]{1,0:T(8,128)(2,1)} %collective-permute-done.3), channel_id=1, source_target_pairs={{0,2},{2,4},{4,6},{6,8},{8,10},{10,12},{12,14},{14,0},{1,3},{3,5},... | collective-permute-start | bytes 1572872 | tf_op jit(solution)/shard_map/ppermute | solution.py:149
  99.9 10.7 %collective-permute-start.5 = (bf16[128,2048]{1,0:T(8,128)(2,1)}, bf16[128,2048]{1,0:T(8,128)(2,1)}, u32[]{:S(2)}, u32[]{:S(2)}) collective-permute-start(bf16[128,2048]{1,0:T(8,128)(2,1)} %collective-permute-done.4), channel_id=1, source_target_pairs={{0,2},{2,4},{4,6},{6,8},{8,10},{10,12},{12,14},{14,0},{1,3},{3,5},... | collective-permute-start | bytes 1572872 | tf_op jit(solution)/shard_map/ppermute | solution.py:149
  110.7 20.2 %collective-permute-start.6 = (bf16[128,2048]{1,0:T(8,128)(2,1)}, bf16[128,2048]{1,0:T(8,128)(2,1)S(1)}, u32[]{:S(2)}, u32[]{:S(2)}) collective-permute-start(bf16[128,2048]{1,0:T(8,128)(2,1)} %collective-permute-done.5), channel_id=1, source_target_pairs={{0,2},{2,4},{4,6},{6,8},{8,10},{10,12},{12,14},{14,0},{1,3},{3,5},... | collective-permute-start | bytes 1572872 | tf_op jit(solution)/shard_map/ppermute | solution.py:149
  123.9 22.9 %copy-start.9 = (bf16[704,2048]{1,0:T(8,128)(2,1)}, bf16[704,2048]{1,0:T(8,128)(2,1)S(1)}, u32[]{:S(2)}) copy-start(bf16[704,2048]{1,0:T(8,128)(2,1)S(1)} %get-tuple-element.9) | copy-start | bytes 8650756
  123.9 26.6 %copy-start.13 = (bf16[704,2048]{1,0:T(8,128)(2,1)}, bf16[704,2048]{1,0:T(8,128)(2,1)S(1)}, u32[]{:S(2)}) copy-start(bf16[704,2048]{1,0:T(8,128)(2,1)S(1)} %get-tuple-element.8) | copy-start | bytes 8650756
  123.9 11.3 %copy-start.19 = (bf16[128,2048]{1,0:T(8,128)(2,1)S(1)}, bf16[128,2048]{1,0:T(8,128)(2,1)}, u32[]{:S(2)}) copy-start(bf16[128,2048]{1,0:T(8,128)(2,1)} %copy-done.18) | copy-start | bytes 1572868
  124.0 11.3 %copy-start.17 = (bf16[128,2048]{1,0:T(8,128)(2,1)S(1)}, bf16[128,2048]{1,0:T(8,128)(2,1)}, u32[]{:S(2)}) copy-start(bf16[128,2048]{1,0:T(8,128)(2,1)} %copy-done.16) | copy-start | bytes 1572868
  135.5 5.9 %slice-start = ((s8[5767168]{0:T(1024)(128)(4,1)}), s8[4194304]{0:T(1024)(128)(4,1)S(1)}, s32[]{:S(2)}) async-start(s8[5767168]{0:T(1024)(128)(4,1)} %bitcast.318), calls=%async_computation.8 | async-start | bytes 8388608
  139.9 1.5 slice-start.1
  141.4 3.4 slice-start.4
  143.1 1.7 slice-start.5
  146.8 1.1 copy-start.32
  150.6 1.0 copy-start.38
  153.8 71.9 %reduce-scatter.7.cloned.1.call-start = ((), (), s32[]{:S(2)}) async-start(), calls=%async_computation.5 | async-start | bytes 2359296 | tf_op jit(solution)/shard_map/reduce_scatter | solution.py:192
  154.2 2.8 copy-start.10
  154.2 2.8 copy-start.33
  160.9 233.7 %reduce-scatter.11.cloned.1.call-start = ((), (), s32[]{:S(2)}) async-start(), calls=%async_computation.7 | async-start | bytes 2359296 | tf_op jit(solution)/shard_map/reduce_scatter | solution.py:192
  227.6 12.1 %collective-permute-start.7 = (bf16[128,2048]{1,0:T(8,128)(2,1)}, bf16[128,2048]{1,0:T(8,128)(2,1)S(1)}, u32[]{:S(2)}, u32[]{:S(2)}) collective-permute-start(bf16[128,2048]{1,0:T(8,128)(2,1)} %add_convert_fusion.5), channel_id=1, source_target_pairs={{0,1},{2,3},{4,5},{6,7},{8,9},{10,11},{12,13},{14,15},{16,17},{18,... | collective-permute-start | bytes 1572872 | tf_op jit(solution)/shard_map/ppermute | solution.py:14
  241.0 3.8 copy-start.3
  241.1 3.8 copy-start.27
  241.1 3.9 copy-start.6
  244.8 4.7 %copy-start.22 = (pred[128,896]{1,0:T(8,128)(4,1)S(1)}, pred[128,896]{1,0:T(8,128)(4,1)}, u32[]{:S(2)}) copy-start(pred[128,896]{1,0:T(8,128)(4,1)} %get-tuple-element.20) | copy-start | bytes 344068
  249.5 6.7 %copy-start.7 = (bf16[768,512]{1,0:T(8,128)(2,1)S(1)}, bf16[768,512]{1,0:T(8,128)(2,1)}, u32[]{:S(2)}) copy-start(bf16[768,512]{1,0:T(8,128)(2,1)} %get-tuple-element.10) | copy-start | bytes 2359300
  249.5 6.7 %copy-start.31 = (bf16[1,8,512,128]{3,2,1,0:T(8,128)(2,1)S(1)}, bf16[1,8,512,128]{3,2,1,0:T(8,128)(2,1)}, u32[]{:S(2)}) copy-start(bf16[1,8,512,128]{3,2,1,0:T(8,128)(2,1)} %param.28) | copy-start | bytes 3145732
  256.2 3.7 copy-start.4
  260.0 66.6 %copy-start.25 = (f32[8,1,64]{2,0,1:T(8,128)S(1)}, f32[8,1,64]{2,0,1:T(8,128)}, u32[]{:S(2)}) copy-start(f32[8,1,64]{2,0,1:T(8,128)} %get-tuple-element.16) | copy-start | bytes 6148
  260.0 66.7 %copy-start.24 = (f32[8,1,64]{2,0,1:T(8,128)S(1)}, f32[8,1,64]{2,0,1:T(8,128)}, u32[]{:S(2)}) copy-start(f32[8,1,64]{2,0,1:T(8,128)} %get-tuple-element.17) | copy-start | bytes 6148
  263.2 10.5 %collective-permute-start.8 = (bf16[128,2048]{1,0:T(8,128)(2,1)S(1)}, bf16[128,2048]{1,0:T(8,128)(2,1)S(1)}, u32[]{:S(2)}, u32[]{:S(2)}) collective-permute-start(bf16[128,2048]{1,0:T(8,128)(2,1)S(1)} %multiply_convert_fusion), channel_id=1, source_target_pairs={{0,2},{2,4},{4,6},{6,8},{8,10},{10,12},{12,14},{14,0},{1,3},{3,5},... | collective-permute-start | bytes 1572872 | tf_op jit(solution)/shard_map/ppermute | solution.py:149
  273.6 10.4 %collective-permute-start.9 = (bf16[128,2048]{1,0:T(8,128)(2,1)S(1)}, bf16[128,2048]{1,0:T(8,128)(2,1)S(1)}, u32[]{:S(2)}, u32[]{:S(2)}) collective-permute-start(bf16[128,2048]{1,0:T(8,128)(2,1)S(1)} %collective-permute-done.8), channel_id=1, source_target_pairs={{0,2},{2,4},{4,6},{6,8},{8,10},{10,12},{12,14},{14,0},{1,3},{3,5},... | collective-permute-start | bytes 1572872 | tf_op jit(solution)/shard_map/ppermute | solution.py:149
  284.0 10.4 %collective-permute-start.10 = (bf16[128,2048]{1,0:T(8,128)(2,1)S(1)}, bf16[128,2048]{1,0:T(8,128)(2,1)S(1)}, u32[]{:S(2)}, u32[]{:S(2)}) collective-permute-start(bf16[128,2048]{1,0:T(8,128)(2,1)S(1)} %collective-permute-done.9), channel_id=1, source_target_pairs={{0,2},{2,4},{4,6},{6,8},{8,10},{10,12},{12,14},{14,0},{1,3},{3,5},... | collective-permute-start | bytes 1572872 | tf_op jit(solution)/shard_map/ppermute | solution.py:149
  294.5 10.4 %collective-permute-start.11 = (bf16[128,2048]{1,0:T(8,128)(2,1)S(1)}, bf16[128,2048]{1,0:T(8,128)(2,1)S(1)}, u32[]{:S(2)}, u32[]{:S(2)}) collective-permute-start(bf16[128,2048]{1,0:T(8,128)(2,1)S(1)} %collective-permute-done.10), channel_id=1, source_target_pairs={{0,2},{2,4},{4,6},{6,8},{8,10},{10,12},{12,14},{14,0},{1,3},{3,5},... | collective-permute-start | bytes 1572872 | tf_op jit(solution)/shard_map/ppermute | solution.py:149
  304.9 10.4 %collective-permute-start.12 = (bf16[128,2048]{1,0:T(8,128)(2,1)S(1)}, bf16[128,2048]{1,0:T(8,128)(2,1)S(1)}, u32[]{:S(2)}, u32[]{:S(2)}) collective-permute-start(bf16[128,2048]{1,0:T(8,128)(2,1)S(1)} %collective-permute-done.11), channel_id=1, source_target_pairs={{0,2},{2,4},{4,6},{6,8},{8,10},{10,12},{12,14},{14,0},{1,3},{3,5},... | collective-permute-start | bytes 1572872 | tf_op jit(solution)/shard_map/ppermute | solution.py:149
  316.1 10.5 %collective-permute-start.13 = (bf16[128,2048]{1,0:T(8,128)(2,1)S(1)}, bf16[128,2048]{1,0:T(8,128)(2,1)}, u32[]{:S(2)}, u32[]{:S(2)}) collective-permute-start(bf16[128,2048]{1,0:T(8,128)(2,1)S(1)} %collective-permute-done.12), channel_id=1, source_target_pairs={{0,2},{2,4},{4,6},{6,8},{8,10},{10,12},{12,14},{14,0},{1,3},{3,5},... | collective-permute-start | bytes 1572872 | tf_op jit(solution)/shard_map/ppermute | solution.py:149
  326.6 10.7 %collective-permute-start.14 = (bf16[128,2048]{1,0:T(8,128)(2,1)}, bf16[128,2048]{1,0:T(8,128)(2,1)}, u32[]{:S(2)}, u32[]{:S(2)}) collective-permute-start(bf16[128,2048]{1,0:T(8,128)(2,1)} %collective-permute-done.13), channel_id=1, source_target_pairs={{0,2},{2,4},{4,6},{6,8},{8,10},{10,12},{12,14},{14,0},{1,3},{3,5},... | collective-permute-start | bytes 1572872 | tf_op jit(solution)/shard_map/ppermute | solution.py:149
  340.9 6.1 %slice-start.2 = ((s8[5767168]{0:T(1024)(128)(4,1)}), s8[4194304]{0:T(1024)(128)(4,1)S(1)}, s32[]{:S(2)}) async-start(s8[5767168]{0:T(1024)(128)(4,1)} %bitcast.320), calls=%async_computation.10 | async-start | bytes 8388608
  345.5 1.5 slice-start.3
  346.2 2.5 slice-start.6
  347.0 2.0 slice-start.7
  349.0 1.9 copy-start.14
  350.9 1.0 copy-start.34
  353.6 1.9 copy-start.11
  355.5 1.0 copy-start.36
  357.3 2.5 copy-start.35
  359.5 2.8 copy-start.37
  359.5 72.0 %reduce-scatter.9.cloned.1.call-start = ((), (), s32[]{:S(2)}) async-start(), calls=%async_computation.6 | async-start | bytes 2359296 | tf_op jit(solution)/shard_map/reduce_scatter | solution.py:192
  359.8 2.5 copy-start.12
  364.1 70.6 %copy-start.1 = (bf16[1,2048,512]{2,1,0:T(8,128)(2,1)S(1)}, bf16[1,2048,512]{2,1,0:T(8,128)(2,1)}, u32[]{:S(2)}) copy-start(bf16[1,2048,512]{2,1,0:T(8,128)(2,1)} %param.30) | copy-start | bytes 6291460
  (2 other events, 1.6 us)
Sparse Core Ops, SparseCore 0:
  153.9 34.6 reduce-scatter.4
  190.9 34.7 reduce-scatter.6
  359.6 34.9 reduce-scatter.10
  396.8 34.7 reduce-scatter.8
